TPU v7x, 32 devices: a whole 2x2x4 slice. The times are simulated.
32 devices in a mesh: row: 4 (over y, x), col: 8 (over z, core).
Axes of the slice: x: 2, y: 2, z: 4, core: 2. Of those that a mesh axis runs over, the one named last changes fastest.
Arguments:
- amps_old: bfloat16 [1024, 262144], P(('row', 'col')), may hold values from -6 to 6
- other_terms: bfloat16 [1024, 262144], P(('row', 'col')), may hold values from -6 to 6
- occ_energy: float32 [32], replicated, may hold values from -1.5 to -0.5
- virt_energy: float32 [512], replicated, may hold values from 0.2 to 1.5
- integrals: bfloat16 [1024, 262144], P('row', 'col'), may hold values from -0.1875 to 0.1875
Outputs:
- amps_new: bfloat16 [1024, 262144], P(('row', 'col'))
All inputs are finite; a program needn't handle non-finite values.
Results may differ from a plain program's by a relative error of at most 0.0055.
Values may be sent and summed in bfloat16 or wider, within the bound.
No kernel may reach another device: no remote copies, remote signals or barrier semaphores. Data moves between devices by JAX's collectives and lax.ppermute only.
A program may use at most 320 MiB of HBM per device.

v0:
```python
import jax
import jax.numpy as jnp
from jax import lax
from jax.sharding import PartitionSpec as P


def pair_energy(pairs, occ_energy):
    count = occ_energy.shape[0]
    first = pairs // count
    second = pairs % count
    grid = jnp.arange(count, dtype=jnp.int32)
    e_first = jnp.sum(jnp.where(first[:, None] == grid[None, :], occ_energy[None, :], 0.0), axis=1)
    e_second = jnp.sum(
        jnp.where(second[:, None] == grid[None, :], occ_energy[None, :], 0.0), axis=1
    )
    return e_first + e_second


def local(amps_old, other_terms, occ_energy, virt_energy, integrals):
    n_row = lax.axis_size("row")
    n_col = lax.axis_size("col")
    row_id = lax.axis_index("row")
    col_id = lax.axis_index("col")
    per_dev = amps_old.shape[0]
    cd_dev = integrals.shape[0]
    window = amps_old[:, : cd_dev * n_row]
    row_pairs = lax.all_gather(window, "col", axis=0, tiled=True)
    panel = lax.all_to_all(row_pairs, "row", split_axis=1, concat_axis=0, tiled=True)
    ladder = lax.psum_scatter(
        jnp.dot(panel, integrals, preferred_element_type=jnp.float32).astype(jnp.bfloat16),
        "row",
        scatter_dimension=0,
        tiled=True,
    ).astype(jnp.float32)
    virt_all = (virt_energy[:, None] + virt_energy[None, :]).reshape(-1)
    first_pair = (row_id * n_col + col_id) * per_dev
    own_pairs = first_pair + jnp.arange(per_dev, dtype=jnp.int32)
    denom_pairs = pair_energy(own_pairs, occ_energy)[:, None] - virt_all[None, :]
    moved = lax.all_to_all(
        ladder.astype(jnp.bfloat16), "col", split_axis=0, concat_axis=1, tiled=True
    ).astype(ladder.dtype)
    increment = (moved / denom_pairs).astype(jnp.bfloat16)
    updated = (
        amps_old.astype(jnp.float32)
        + other_terms.astype(jnp.float32) / denom_pairs
        + increment.astype(jnp.float32)
    )
    return updated.astype(jnp.bfloat16)


def solution(mesh):
    return jax.shard_map(
        local,
        mesh=mesh,
        in_specs=(P(("row", "col"), None), P(("row", "col"), None), P(), P(), P("row", "col")),
        out_specs=P(("row", "col"), None),
        check_vma=False,
    )
```

profile of v0, /device:TPU:0, one launch (start us, length us, event | category | flops | bytes accessed | tf_op | source)
XLA Modules:
  0.0 1049.0 jit_solution(17985617899202413814)
XLA Ops:
  6.5 0.0 reduce-scatter.4.cloned.1.call-start
  6.5 0.8 slice.3
  7.4 16.5 %all_gather.3 = bf16[256,1024]{1,0:T(8,128)(2,1)S(1)} all-gather(bf16[32,1024]{1,0:T(8,128)(2,1)S(1)} %slice.3), channel_id=1, replica_groups=mesh['row'=4,'col'=8] {'col'}, dimensions={0}, use_global_device_ids=true | all-gather | bytes 589824 | tf_op jit(solution)/shard_map/all_gather | solution.py:27
  23.9 0.2 copy.14
  24.1 12.5 %all_to_all.32 = bf16[256,4,256]{0,2,1:T(8,128)(2,1)S(1)} all-to-all(bf16[256,4,256]{0,2,1:T(8,128)(2,1)S(1)} %bitcast.18), channel_id=1, replica_groups=mesh['row'=4,'col'=8] {'row'}, dimensions={1} | all-to-all | bytes 1048576 | tf_op jit(solution)/shard_map/all_to_all | solution.py:28
  36.6 0.2 copy.15
  36.8 30.6 %convolution_convert_fusion = bf16[1024,32768]{1,0:T(8,128)(2,1)} fusion(bf16[1024,256]{1,0:T(8,128)(2,1)S(1)} %bitcast.16, bf16[256,32768]{1,0:T(8,128)(2,1)} %param.9), kind=kOutput, calls=%fused_computation | convolution fusion | flops 17213423616 | bytes 84410368 | tf_op jit(solution)/shard_map/dot_general | solution.py:30
  67.4 0.0 reduce-scatter.4.cloned.1.call-update
  67.4 0.0 copy-start
  67.4 0.0 copy-start.1
  67.5 557.9 %reduce-scatter.4.cloned.1.call-done = bf16[256,32768]{1,0:T(8,128)(2,1)} async-done(((bf16[1024,32768]{1,0:T(8,128)(2,1)}), bf16[256,32768]{1,0:T(8,128)(2,1)}) %reduce-scatter.4.cloned.1.call-update) | async-done | bytes 16777232
  625.4 5.8 all-to-all-start.1
  631.1 0.0 copy-done
  631.1 0.1 add_bitcast_fusion
  631.3 0.3 copy.18
  631.6 0.0 copy-done.1
  631.6 0.2 select_reduce_fusion
  631.8 363.0 %all-to-all-done.1 = bf16[8,32,32768]{2,1,0:T(8,128)(2,1)} async-done(((bf16[8,32,32768]{2,1,0:T(8,128)(2,1)}), bf16[8,32,32768]{2,1,0:T(8,128)(2,1)}, u32[]{:S(2)}, u32[]{:S(2)}) %all-to-all-start.1) | async-done | bytes 16777248 | tf_op jit(solution)/shard_map/all_to_all | solution.py:39
  994.8 8.5 convert_bitcast_fusion
  1003.3 11.2 %copy.17 = f32[8,4,8,32768]{3,2,0,1:T(8,128)} copy(f32[8,4,8,32768]{3,2,1,0:T(8,128)S(1)} %convert_bitcast_fusion) | data formatting | bytes 67108864 | tf_op jit(solution)/shard_map/convert_element_type | solution.py:41
  1014.5 27.6 %fusion.3 = bf16[32,262144]{1,0:T(8,128)(2,1)} fusion(bf16[32,262144]{1,0:T(8,128)(2,1)} %param.6, bf16[32,262144]{1,0:T(8,128)(2,1)} %param.5, f32[32,262144]{1,0:T(8,128)} %bitcast.14, f32[262144]{0:T(1024)S(1)} %bitcast.17, f32[32]{0:T(128)S(1)} %add.70), kind=kLoop, calls=%fused_computation.7 | loop fusion | flops 83886080 | bytes 84934784 | tf_op jit(solution)/shard_map/convert_element_type | solution.py:48
  (2 shorter events, 0.0 us)
Async XLA Ops:
  6.5 618.8 %reduce-scatter.4.cloned.1.call-start = ((), (), s32[]{:S(2)}) async-start(), calls=%async_computation.3 | async-start | bytes 83886080
  67.4 563.7 %copy-start = (f32[512]{0:T(512)S(1)}, f32[512]{0:T(512)}, u32[]{:S(2)}) copy-start(f32[512]{0:T(512)} %param.8) | copy-start | bytes 6148
  67.4 564.1 %copy-start.1 = (f32[32]{0:T(128)S(1)}, f32[32]{0:T(128)}, u32[]{:S(2)}) copy-start(f32[32]{0:T(128)} %param.7) | copy-start | bytes 388
  625.4 369.4 %all-to-all-start.1 = ((bf16[8,32,32768]{2,1,0:T(8,128)(2,1)}), bf16[8,32,32768]{2,1,0:T(8,128)(2,1)}, u32[]{:S(2)}, u32[]{:S(2)}) async-start(bf16[8,32,32768]{2,1,0:T(8,128)(2,1)} %bitcast.15), calls=%async_computation.1 | async-start | bytes 33554432 | tf_op jit(solution)/shard_map/all_to_all | solution.py:39
Sparse Core Ops, SparseCore 0:
  67.6 557.7 reduce-scatter.3
where the time goes:
time: 1050 us
  waiting for transfers between devices  921 us (88%)
  other arithmetic  36.5 us (3%)
  matrix products  30.6 us (3%)
  blocking collectives  29 us (3%)
  between operations  13.5 us (1%)
  local copies, waits for them, and re-layouts  12.7 us (1%)
    unnamed x2, waiting for transfers between devices  558 us
    all_to_all x1, waiting for transfers between devices, local(): lax.all_to_all(ladder.astype(jnp.bfloat16), 'col', split_axis=0, concat_a...  363 us
    dot_general x1, matrix products, local(): jnp.dot(panel, integrals, preferred_element_type=jnp.float32)  30.6 us
    convert_element_type x1, other arithmetic, local(): return updated.astype(jnp.bfloat16)  27.6 us
  transfers between devices with their start and end apart: 2, of which 2 were waited for; matrix products, arithmetic and copies ran while one was open for 0% of the time, Pallas kernels for 0%

commit v1 on v0

--- a/solution.py
+++ b/solution.py
@@ -36,8 +36,14 @@
     first_pair = (row_id * n_col + col_id) * per_dev
     own_pairs = first_pair + jnp.arange(per_dev, dtype=jnp.int32)
     denom_pairs = pair_energy(own_pairs, occ_energy)[:, None] - virt_all[None, :]
-    moved = lax.all_to_all(
-        ladder.astype(jnp.bfloat16), "col", split_axis=0, concat_axis=1, tiled=True
+    moved = jnp.concatenate(
+        lax.all_to_all(
+            jnp.stack(jnp.split(ladder.astype(jnp.bfloat16), lax.axis_size("col"), axis=0)),
+            "col",
+            0,
+            0,
+        ),
+        axis=1,
     ).astype(ladder.dtype)
     increment = (moved / denom_pairs).astype(jnp.bfloat16)
     updated = (

time: 1050 us -> 1640 us (1.56)
  waiting for transfers between devices: 921 us -> 1480 us
  local copies, waits for them, and re-layouts: 12.7 us -> 42 us
    unnamed x2, waiting for transfers between devices: 558 us -> 1110 us
    unnamed x5 -> x15, local copies, waits for them, and re-layouts: 0.28 us -> 25.9 us
where the time goes in v1:
time: 1640 us
  waiting for transfers between devices  1480 us (90%)
  local copies, waits for them, and re-layouts  42 us (3%)
  other arithmetic  36.5 us (2%)
  matrix products  30.7 us (2%)
  blocking collectives  29 us (2%)
    unnamed x2, waiting for transfers between devices  1110 us
    all_to_all x1, waiting for transfers between devices, local(): lax.all_to_all(jnp.stack(jnp.split(ladder.astype(jnp.bfloat16), lax.axis_...  363 us
  transfers between devices with their start and end apart: 2, of which 2 were waited for; matrix products, arithmetic and copies ran while one was open for 0% of the time, Pallas kernels for 0%

profile of v1, /device:TPU:0, one launch (start us, length us, event | category | flops | bytes accessed | tf_op | source)
XLA Modules:
  0.0 1635.9 jit_solution(11836754688429700646)
XLA Ops:
  6.5 0.0 all-reduce.3.cloned.1.call-start
  6.5 0.8 slice.3
  7.4 16.5 %all_gather.3 = bf16[256,1024]{1,0:T(8,128)(2,1)S(1)} all-gather(bf16[32,1024]{1,0:T(8,128)(2,1)S(1)} %slice.3), channel_id=1, replica_groups=mesh['row'=4,'col'=8] {'col'}, dimensions={0}, use_global_device_ids=true | all-gather | bytes 589824 | tf_op jit(solution)/shard_map/all_gather | solution.py:27
  23.9 0.2 copy.13
  24.1 12.5 all_to_all.24
  36.6 0.2 copy.14
  36.8 30.7 %convolution_convert_fusion = bf16[1024,32768]{1,0:T(8,128)(2,1)} fusion(bf16[1024,256]{1,0:T(8,128)(2,1)S(1)} %bitcast.46, bf16[256,32768]{1,0:T(8,128)(2,1)} %param.9), kind=kOutput, calls=%fused_computation | convolution fusion | flops 17213423616 | bytes 84410368 | tf_op jit(solution)/shard_map/dot_general | solution.py:30
  67.5 0.0 copy-start.2
  67.5 0.0 all-reduce.3.cloned.1.call-update
  67.6 0.6 copy-done.2
  68.2 0.6 dynamic-slice
  69.4 1114.7 %all-reduce.3.cloned.1.call-done = bf16[1024,32768]{1,0:T(8,128)(2,1)} async-done(((bf16[1024,32768]{1,0:T(8,128)(2,1)}), bf16[1024,32768]{1,0:T(8,128)(2,1)}) %all-reduce.3.cloned.1.call-update) | async-done | bytes 67108880
  1184.1 3.0 fusion.11
  1187.1 3.6 fusion.10
  1190.7 3.6 fusion.9
  1194.3 3.6 fusion.8
  1197.8 3.6 fusion.7
  1201.4 3.6 fusion.6
  1205.0 3.6 fusion.5
  1208.5 3.6 fusion.4
  1212.1 0.0 copy-start
  1212.1 0.0 copy-start.1
  1212.1 5.9 all-to-all-start.1
  1218.0 0.0 copy-done
  1218.0 0.1 add_bitcast_fusion
  1218.1 0.3 copy.17
  1218.5 0.0 copy-done.1
  1218.5 0.2 select_reduce_fusion
  1218.7 363.0 %all-to-all-done.1 = bf16[8,32,32768]{2,1,0:T(8,128)(2,1)} async-done(((bf16[8,32,32768]{2,1,0:T(8,128)(2,1)}), bf16[8,32,32768]{2,1,0:T(8,128)(2,1)}, u32[]{:S(2)}, u32[]{:S(2)}) %all-to-all-start.1) | async-done | bytes 16777248 | tf_op jit(solution)/shard_map/all_to_all | solution.py:40
  1581.6 8.5 convert_bitcast_fusion
  1590.2 11.2 copy.16
  1601.4 27.6 %fusion.3 = bf16[32,262144]{1,0:T(8,128)(2,1)} fusion(bf16[32,262144]{1,0:T(8,128)(2,1)} %param.6, bf16[32,262144]{1,0:T(8,128)(2,1)} %param.5, f32[32,262144]{1,0:T(8,128)} %bitcast.45, f32[262144]{0:T(1024)S(1)} %bitcast.47, f32[32]{0:T(128)S(1)} %add.70), kind=kLoop, calls=%fused_computation.7 | loop fusion | flops 83886080 | bytes 84934784 | tf_op jit(solution)/shard_map/convert_element_type | solution.py:54
  (2 shorter events, 0.0 us)
Async XLA Ops:
  6.5 1177.6 %all-reduce.3.cloned.1.call-start = ((), (), s32[]{:S(2)}) async-start(), calls=%async_computation.2 | async-start | bytes 134217728
  67.5 0.7 copy-start.2
  1212.1 5.9 copy-start
  1212.1 6.4 copy-start.1
  1212.1 369.5 %all-to-all-start.1 = ((bf16[8,32,32768]{2,1,0:T(8,128)(2,1)}), bf16[8,32,32768]{2,1,0:T(8,128)(2,1)}, u32[]{:S(2)}, u32[]{:S(2)}) async-start(bf16[8,32,32768]{2,1,0:T(8,128)(2,1)} %fusion.4), calls=%async_computation.1 | async-start | bytes 33554432 | tf_op jit(solution)/shard_map/all_to_all | solution.py:40
Sparse Core Ops, SparseCore 0:
  67.7 1116.3 all-reduce.2
